TPU v7x, 32 devices: a whole 2x2x4 slice. The times are simulated.
32 devices in a mesh: design: 8 (over z, x), feat: 4 (over y, core).
Axes of the slice: x: 2, y: 2, z: 4, core: 2. Of those that a mesh axis runs over, the one named last changes fastest.
Arguments:
- table: bfloat16 [32768, 1024], P('design', 'feat'), may hold values from -0.29882812 to 0.29882812
- proj_weight: float32 [1024, 128], P('feat'), may hold values from -0.1875 to 0.1875
- anchor_ids: int32 [4096], P('design'), may hold values from 0 to 32767, as said below
- positive_ids: int32 [4096], P('design'), may hold values from 0 to 32767, as said below
- neg_tiles: int32 [32, 16], P('design'), may hold values from 0 to 255, as said below
Outputs:
- losses: float32 [4096], P('design')
- table_grad: float32 [32768, 1024], P('design', 'feat')
- weight_grad: float32 [1024, 128], P('feat')
Inputs may be any that keep to these rules, and one draw needn't show every extreme that they name: `anchor_ids`: entry i lies in the rows held by design index i // 512, that is from that index times 4096 on, 4096 rows. `positive_ids`: entry i lies in the rows held by design index i // 512, that is from that index times 4096 on, 4096 rows. `neg_tiles`: tile t is held by design index t // 32. Among the 4 rows of blocks of one design index, at most 16 entries name tiles held by any one index, and exactly 16 for some index.
All inputs are finite; a program needn't handle non-finite values.
Results may differ from a plain program's by a relative error of at most 0.0004.
Values may be sent and summed in bfloat16 or wider, within the bound.
A program may use at most 192 MiB of HBM per device.

v0:
```python
import jax
import jax.numpy as jnp
from jax import lax
from jax.sharding import PartitionSpec as P

TILE = 128
SOFTMAX_TEMP = 0.07
EPSILON = 1e-06


def unit_rows(values):
    return values / jnp.sqrt(jnp.sum(values * values, axis=-1, keepdims=True) + EPSILON)


def block_losses(anchor_z, positive_z, negative_z):
    anchor_unit_vector = unit_rows(anchor_z)
    positive_unit_vector = unit_rows(positive_z)
    negative_unit_vector = unit_rows(negative_z)
    positive_similarity = jnp.sum(anchor_unit_vector * positive_unit_vector, axis=-1) / SOFTMAX_TEMP
    negative_similarity = (
        jnp.einsum(
            "kjc,koc->kjo",
            anchor_unit_vector,
            negative_unit_vector,
            precision=lax.Precision.HIGHEST,
        )
        / SOFTMAX_TEMP
    )
    total = jnp.exp(positive_similarity) + jnp.sum(jnp.exp(negative_similarity), axis=-1)
    return jnp.log(total) - positive_similarity


def full_dot(left, right):
    return jnp.dot(left, right, precision=lax.Precision.HIGHEST, preferred_element_type=jnp.float32)


def shards(table, proj_weight, anchor_ids, positive_ids, neg_tiles):
    n_design = lax.axis_size("design")
    my_index = lax.axis_index("design")
    shard_rows, width = table.shape
    code_width = proj_weight.shape[1]
    tiles_dev = shard_rows // TILE
    blocks, negs = neg_tiles.shape
    wanted = blocks * negs
    capacity = 2 * wanted // n_design
    slot_count = n_design * capacity
    anchor_local = anchor_ids - my_index * shard_rows
    positive_local = positive_ids - my_index * shard_rows
    flat_tiles = neg_tiles.reshape(wanted)
    owner_dev = flat_tiles // tiles_dev
    local_tile = flat_tiles - owner_dev * tiles_dev
    request_order = jnp.arange(wanted, dtype=jnp.int32)
    earlier = (owner_dev[:, None] == owner_dev[None, :]) & (
        request_order[:, None] < request_order[None, :]
    )
    slot_rank = jnp.sum(earlier.astype(jnp.int32), axis=0)
    slot_position = owner_dev * capacity + slot_rank
    request = jnp.zeros((slot_count,), jnp.int32).at[slot_position].set(local_tile)
    asked = lax.all_to_all(
        request.reshape(n_design, capacity), "design", split_axis=0, concat_axis=0, tiled=True
    ).reshape(slot_count)
    own_embed = table.astype(jnp.float32)
    anchor_part = full_dot(own_embed[anchor_local], proj_weight)
    positive_part = full_dot(own_embed[positive_local], proj_weight)
    anchor_z, positive_z = lax.psum((anchor_part, positive_part), "feat")
    outgoing = table.reshape(tiles_dev, TILE, width)[asked].reshape(n_design, capacity, TILE, width)
    arrived = lax.all_to_all(outgoing, "design", split_axis=0, concat_axis=0, tiled=True).reshape(
        slot_count, TILE, width
    )
    negative_embed = arrived[slot_position].reshape(wanted * TILE, width).astype(jnp.float32)
    negative_z = lax.psum(full_dot(negative_embed, proj_weight), "feat")
    losses, pullback = jax.vjp(
        block_losses,
        anchor_z.reshape(blocks, TILE, code_width),
        positive_z.reshape(blocks, TILE, code_width),
        negative_z.reshape(blocks, negs * TILE, code_width),
    )
    anchor_grad, positive_grad, negative_grad = pullback(jnp.ones_like(losses))
    code_grad = jnp.zeros((shard_rows, code_width), jnp.float32)
    code_grad = code_grad.at[anchor_local].add(anchor_grad.reshape(-1, code_width))
    code_grad = code_grad.at[positive_local].add(positive_grad.reshape(-1, code_width))
    negative_tiles_grad = negative_grad.reshape(wanted, TILE, code_width)
    negative_rows_grad = negative_tiles_grad.reshape(wanted * TILE, code_width)
    embed_grad = full_dot(negative_rows_grad, proj_weight.T).reshape(wanted, TILE, width)
    weight_part = full_dot(own_embed.T, code_grad) + full_dot(negative_embed.T, negative_rows_grad)
    send_back = jnp.zeros((slot_count, TILE, width), jnp.float32).at[slot_position].set(embed_grad)
    returned = lax.all_to_all(
        send_back.reshape(n_design, capacity, TILE, width).astype(jnp.bfloat16),
        "design",
        split_axis=0,
        concat_axis=0,
        tiled=True,
    ).astype(jnp.float32)
    table_grad = full_dot(code_grad, proj_weight.T).reshape(tiles_dev, TILE, width)
    table_grad = (
        table_grad.at[asked]
        .add(returned.reshape(slot_count, TILE, width))
        .reshape(shard_rows, width)
    )
    weight_grad = lax.psum(weight_part, "design")
    return (losses.reshape(blocks * TILE), table_grad, weight_grad)


def solution(mesh):
    in_specs = (P("design", "feat"), P("feat", None), P("design"), P("design"), P("design", None))
    out_specs = (P("design"), P("design", "feat"), P("feat", None))
    return jax.shard_map(shards, mesh=mesh, in_specs=in_specs, out_specs=out_specs, check_vma=False)
```

profile of v0, /device:TPU:8, one launch (start us, length us, event | category | flops | bytes accessed | tf_op | source)
XLA Modules:
  0.0 666.7 jit_solution(4649962688690059816)
XLA Ops:
  9.8 11.1 %all_to_all.19 = s32[8,1,16]{2,1,0:T(1,128)S(1)} all-to-all(s32[8,1,16]{2,1,0:T(1,128)S(1)} %bitcast.88), channel_id=1, replica_groups=mesh['design'=8,'feat'=4] {'design'}, dimensions={0} | all-to-all | bytes 1024 | tf_op jit(solution)/shard_map/all_to_all | solution.py:59
  22.2 6.2 gather_fusion.2
  28.4 6.6 all-to-all-start.1
  35.1 2.0 gather_fusion
  37.1 2.0 gather_fusion.1
  40.1 1.1 fusion.33
  41.2 173.3 %all-to-all-done.1 = bf16[8,16,128,256]{3,2,1,0:T(8,128)(2,1)} async-done(((bf16[8,16,128,256]{3,2,1,0:T(8,128)(2,1)}), bf16[8,16,128,256]{3,2,1,0:T(8,128)(2,1)}, u32[]{:S(2)}, u32[]{:S(2)}) %all-to-all-start.1) | async-done | bytes 8388640 | tf_op jit(solution)/shard_map/all_to_all | solution.py:67
  214.5 6.2 gather_fusion.3
  220.7 7.5 %fusion.34 = f32[8192,128]{1,0:T(8,128)} fusion(bf16[8192,256]{1,0:T(8,128)(2,1)} %bitcast.74, f32[256,128]{1,0:T(8,128)S(1)} %copy-done.7), kind=kOutput, calls=%fused_computation.98 | convolution fusion | flops 3221225472 | bytes 8519680 | tf_op jit(solution)/shard_map/dot_general | solution.py:34
  228.3 95.3 %all-reduce.6.cloned.1.call-done = (f32[8192,128]{1,0:T(8,128)}, f32[512,128]{1,0:T(8,128)}, f32[512,128]{1,0:T(8,128)}) async-done(((f32[8192,128]{1,0:T(8,128)}, f32[512,128]{1,0:T(8,128)}, f32[512,128]{1,0:T(8,128)}), (f32[8192,128]{1,0:T(8,128)}, f32[512,128]{1,0:T(8,128)}, f32[512,128]{1,0:T(8,128)})) %all-reduce.6.cloned.1.call-update) | async-done | bytes 4718608 | tf_op jit(solution)/shard_map/psum | solution.py:71
  323.6 1.2 multiply_reduce_fusion.6
  324.8 1.1 multiply_reduce_fusion.5
  325.9 3.3 multiply_reduce_fusion.1
  329.7 7.1 %fusion = (f32[4,128]{1,0:T(4,128)S(1)}, f32[4,128,2048]{2,1,0:T(8,128)S(1)}) fusion(f32[4,2048,128]{2,1,0:T(8,128)} %bitcast.78, f32[4,2048]{1,0:T(4,128)S(1)} %sqrt.60, f32[4,128,128]{2,1,0:T(8,128)S(1)} %bitcast.83, f32[4,128]{1,0:T(4,128)S(1)} %get-tuple-element.28), kind=kOutput, calls=%fused_computation.15 | convolution fusion | flops 1613823488 | bytes 8687616 | tf_op jit(solution)/shard_map/jvp(kjc,koc->kjo)/dot_general | solution.py:21
  336.8 9.8 %multiply_reduce_fusion = (f32[4,2048]{1,0:T(4,128)S(1)}, f32[4,2048,128]{2,1,0:T(8,128)S(1)}) fusion(f32[4,2048,128]{2,1,0:T(8,128)S(1)} %bitcast.80, f32[4,2048]{1,0:T(4,128)S(1)} %multiply_divide_fusion, f32[4,128,128]{2,1,0:T(8,128)S(1)} %bitcast.84, f32[4,128]{1,0:T(4,128)S(1)} %get-tuple-element.28, f32[4,128,2048]{2,1,0:T(8,128)S(1)} %get-tuple-element.30, ...), kind=kOutput, calls=%fused_computation.11 | convolution fusion | flops 1616961536 | bytes 12914688 | tf_op jit(solution)/shard_map/transpose(jvp(kjc,koc->kjo))/dot_general | solution.py:21
  346.7 2.5 add_add_fusion
  349.2 1.9 copy-done.2
  351.1 8.9 %fusion.15 = f32[64,128,256]{2,1,0:T(8,128)} fusion(f32[64,128,128]{2,1,0:T(8,128)S(1)} %bitcast.76, f32[256,128]{1,0:T(8,128)S(1)} %copy-done.7), kind=kOutput, calls=%fused_computation.40 | convolution fusion | flops 3221225472 | bytes 12713984 | tf_op jit(solution)/shard_map/dot_general | solution.py:34
  360.0 7.8 %broadcast_in_dim.61 = f32[128,128,256]{2,1,0:T(8,128)} broadcast(f32[]{:T(128)} %constant.21.clone.1), dimensions={} | broadcast | bytes 16777220 | tf_op jit(solution)/shard_map/broadcast_in_dim | solution.py:86
  367.9 16.1 %scatter_fusion = f32[128,128,256]{2,1,0:T(8,128)} fusion(f32[128,128,256]{2,1,0:T(8,128)} %broadcast_in_dim.61, s32[64]{0:T(128)S(1)} %fusion.24, f32[64,128,256]{2,1,0:T(8,128)} %fusion.15), kind=kCustom, calls=%fused_computation.7 | custom fusion | bytes 25166080 | tf_op jit(solution)/shard_map/scatter | solution.py:86
  384.0 9.0 %convert_element_type.13 = bf16[128,128,256]{2,1,0:T(8,128)(2,1)} convert(f32[128,128,256]{2,1,0:T(8,128)} %scatter_fusion) | non-fusion elementwise | flops 4194304 | bytes 25165824 | tf_op jit(solution)/shard_map/convert_element_type | solution.py:88
  392.9 6.2 all-to-all-start.2
  400.2 8.0 %multiply_reduce_fusion.3 = (f32[4,128]{1,0:T(4,128)S(1)}, f32[4,128,128]{2,1,0:T(8,128)S(1)}) fusion(f32[4,128,128]{2,1,0:T(8,128)S(1)} %bitcast.85, f32[4,128]{1,0:T(4,128)S(1)} %multiply_divide_fusion.2, f32[4,128,128]{2,1,0:T(8,128)S(1)} %bitcast.86, f32[4,128]{1,0:T(4,128)S(1)} %get-tuple-element.24, f32[4,128]{1,0:T(4,128)S(1)} %get-tuple-element.21, ...), kind=kOutput, calls=%fused_computation.35 | convolution fusion | flops 1615199744 | bytes 9218048 | tf_op jit(solution)/shard_map/transpose(jvp(kjc,koc->kjo))/dot_general | solution.py:21
  408.4 3.6 scatter_custom_fusion.1
  412.1 6.4 scatter_custom_fusion.2
  418.5 3.5 convolution_bitcast_fusion
  422.0 6.4 convolution_add_fusion
  428.5 7.0 %fusion.35 = f32[4096,256]{1,0:T(8,128)} fusion(f32[4096,128]{1,0:T(8,128)} %scatter_custom_fusion.2, f32[256,128]{1,0:T(8,128)S(1)} %copy-done.7), kind=kOutput, calls=%fused_computation.99 | convolution fusion | flops 1610612736 | bytes 6422528 | tf_op jit(solution)/shard_map/dot_general | solution.py:34
  435.6 168.4 %all-reduce.4.cloned.1.call-done = f32[256,128]{0,1:T(8,128)} async-done(((f32[256,128]{0,1:T(8,128)}), f32[256,128]{0,1:T(8,128)}) %all-reduce.4.cloned.1.call-update) | async-done | bytes 131088 | tf_op jit(solution)/shard_map/psum | solution.py:100
  603.9 1.7 copy.18
  605.6 11.5 %bitcast_convert_fusion = f32[128,128,256]{2,1,0:T(8,128)} fusion(bf16[8,16,128,256]{3,2,1,0:T(8,128)(2,1)} %all-to-all-done.2), kind=kLoop, calls=%fused_computation.9 | loop fusion | flops 4194304 | bytes 25165824 | tf_op jit(solution)/shard_map/reshape | solution.py:97
  617.0 42.6 %scatter_fusion.1 = f32[32,128,256]{2,1,0:T(8,128)} fusion(f32[32,128,256]{2,1,0:T(8,128)} %bitcast.72, s32[128]{0:T(128)S(1)} %fusion.25, f32[128,128,256]{2,1,0:T(8,128)} %bitcast_convert_fusion), kind=kCustom, calls=%fused_computation.8 | custom fusion | flops 4194304 | bytes 50332160 | tf_op jit(solution)/shard_map/scatter-add | solution.py:97
  (56 shorter events, 6.7 us)
Async XLA Ops:
  7.2 15.0 %copy-start = (bf16[4096,256]{1,0:T(8,128)(2,1)S(1)}, bf16[4096,256]{1,0:T(8,128)(2,1)}, u32[]{:S(2)}) copy-start(bf16[4096,256]{1,0:T(8,128)(2,1)} %param.5) | copy-start | bytes 6291460
  28.4 6.7 copy-start.8
  28.4 6.7 copy-start.9
  28.4 186.1 %all-to-all-start.1 = ((bf16[8,16,128,256]{3,2,1,0:T(8,128)(2,1)}), bf16[8,16,128,256]{3,2,1,0:T(8,128)(2,1)}, u32[]{:S(2)}, u32[]{:S(2)}) async-start(bf16[8,16,128,256]{3,2,1,0:T(8,128)(2,1)} %bitcast.82), calls=%async_computation.1 | async-start | bytes 16777216 | tf_op jit(solution)/shard_map/all_to_all | solution.py:67
  35.1 4.0 copy-start.7
  35.1 288.5 %all-reduce.6.cloned.1.call-start = ((), (), s32[]{:S(2)}) async-start(), calls=%async_computation.4 | async-start | bytes 9437184 | tf_op jit(solution)/shard_map/psum | solution.py:71
  323.6 5.7 copy-start.4
  323.6 5.8 copy-start.5
  329.6 7.2 %copy-start.3 = (f32[8192,128]{1,0:T(8,128)S(1)}, f32[8192,128]{1,0:T(8,128)}, u32[]{:S(2)}) copy-start(f32[8192,128]{1,0:T(8,128)} %get-tuple-element.12) | copy-start | bytes 12582916
  336.8 9.9 %copy-start.6 = (f32[4,128,2048]{2,1,0:T(8,128)}, f32[4,128,2048]{2,1,0:T(8,128)S(1)}, u32[]{:S(2)}) copy-start(f32[4,128,2048]{2,1,0:T(8,128)S(1)} %get-tuple-element.30) | copy-start | bytes 12582916
  349.2 1.9 copy-start.2
  392.9 212.6 %all-to-all-start.2 = ((bf16[8,16,128,256]{3,2,1,0:T(8,128)(2,1)}), bf16[8,16,128,256]{3,2,1,0:T(8,128)(2,1)}, u32[]{:S(2)}, u32[]{:S(2)}) async-start(bf16[8,16,128,256]{3,2,1,0:T(8,128)(2,1)} %bitcast.81), calls=%async_computation.2 | async-start | bytes 16777216 | tf_op jit(solution)/shard_map/all_to_all | solution.py:87
  399.2 204.7 %all-reduce.4.cloned.1.call-start = ((), (), s32[]{:S(2)}) async-start(), calls=%async_computation.3 | async-start | bytes 262144 | tf_op jit(solution)/shard_map/psum | solution.py:100
  418.5 3.6 copy-start.1
Sparse Core Ops, SparseCore 0:
  228.4 95.0 all-reduce.5
  428.6 175.2 all-reduce.3
where the time goes:
time: 676 us; the launch traced here: 667 us
  waiting for transfers between devices  437 us (65%)
  other arithmetic  83.6 us (12%)
  matrix products  60.6 us (9%)
  local copies, waits for them, and re-layouts  47 us (7%)
  between operations  14.6 us (2%)
  starting transfers between devices  12.9 us (2%)
  blocking collectives  11.1 us (2%)
    all_to_all x1, waiting for transfers between devices, shards(): lax.all_to_all(outgoing, 'design', split_axis=0, concat_axis=0, tiled=True)  173 us
    psum x1, waiting for transfers between devices, shards(): weight_grad = lax.psum(weight_part, 'design')  168 us
    psum x1, waiting for transfers between devices, shards(): negative_z = lax.psum(full_dot(negative_embed, proj_weight), 'feat')  95.3 us
    scatter-add x1, other arithmetic, shards(): table_grad = table_grad.at[asked].add(returned.reshape(slot_count, TILE,...  42.6 us
    dot_general x7, matrix products, full_dot(): jnp.dot(left, right, precision=lax.Precision.HIGHEST, preferred_element_t...  35.6 us
    dot_general x3, matrix products, block_losses(): jnp.einsum('kjc,koc->kjo', anchor_unit_vector, negative_unit_vector, prec...  25 us
    scatter x1, local copies, waits for them, and re-layouts, shards(): jnp.zeros((slot_count, TILE, width), jnp.float32).at[slot_position]  16.1 us
  transfers between devices with their start and end apart: 4, of which 3 were waited for; matrix products, arithmetic and copies ran while one was open for 7% of the time, Pallas kernels for 0%

commit v1 on v0

--- a/solution.py
+++ b/solution.py
@@ -97,7 +97,19 @@
         .add(returned.reshape(slot_count, TILE, width))
         .reshape(shard_rows, width)
     )
-    weight_grad = lax.psum(weight_part, "design")
+
+    def patches_create(work_x):
+        e_next = work_x
+        n_shards = lax.axis_size("design")
+        for hop_no in [i for i in (1, 2, 4, 8, 16) if i < n_shards]:
+            view_out = range(n_shards)
+            long_array = map(lambda dd: (dd, dd ^ hop_no), view_out)
+            outer = list(long_array)
+            tile_out = lax.ppermute(e_next, axis_name="design", perm=outer)
+            e_next = e_next + tile_out
+        return e_next
+
+    weight_grad = patches_create(weight_part)
     return (losses.reshape(blocks * TILE), table_grad, weight_grad)
 
 

time: 676 us -> 655 us (0.969)
  waiting for transfers between devices: 437 us -> 417 us
    psum x1 -> x0, waiting for transfers between devices: 168 us -> none  [shards(): weight_grad = lax.psum(weight_part, 'design')]
    ppermute x0 -> x3, waiting for transfers between devices: none -> 148 us  [patches_create(): tile_out = lax.ppermute(e_next, axis_name='design', perm=outer)]
  transfers between devices with their start and end apart: 4 -> 6, of which waited for: 3 -> 5; matrix products, arithmetic and copies ran while one was open for 7% -> 6% of each run, Pallas kernels for 0% -> 0%
where the time goes in v1:
time: 655 us; the launch traced here: 646 us
  waiting for transfers between devices  417 us (64%)
  other arithmetic  82.7 us (13%)
  matrix products  57.8 us (9%)
  local copies, waits for them, and re-layouts  46.1 us (7%)
  starting transfers between devices  16.9 us (3%)
  between operations  14.6 us (2%)
  blocking collectives  11.1 us (2%)
    all_to_all x1, waiting for transfers between devices, shards(): lax.all_to_all(outgoing, 'design', split_axis=0, concat_axis=0, tiled=True)  173 us
    ppermute x3, waiting for transfers between devices, patches_create(): tile_out = lax.ppermute(e_next, axis_name='design', perm=outer)  148 us
    psum x1, waiting for transfers between devices, shards(): negative_z = lax.psum(full_dot(negative_embed, proj_weight), 'feat')  95.3 us
    scatter-add x1, other arithmetic, shards(): table_grad = table_grad.at[asked].add(returned.reshape(slot_count, TILE,...  42.6 us
    dot_general x7, matrix products, full_dot(): jnp.dot(left, right, precision=lax.Precision.HIGHEST, preferred_element_t...  33 us
    dot_general x3, matrix products, block_losses(): jnp.einsum('kjc,koc->kjo', anchor_unit_vector, negative_unit_vector, prec...  24.8 us
    scatter x1, local copies, waits for them, and re-layouts, shards(): jnp.zeros((slot_count, TILE, width), jnp.float32).at[slot_position]  16.1 us
  transfers between devices with their start and end apart: 6, of which 5 were waited for; matrix products, arithmetic and copies ran while one was open for 6% of the time, Pallas kernels for 0%

profile of v1, /device:TPU:8, one launch (start us, length us, event | category | flops | bytes accessed | tf_op | source)
XLA Modules:
  0.0 646.1 jit_solution(11937054193899511719)
XLA Ops:
  9.8 11.1 %all_to_all.19 = s32[8,1,16]{2,1,0:T(1,128)S(1)} all-to-all(s32[8,1,16]{2,1,0:T(1,128)S(1)} %bitcast.86), channel_id=1, replica_groups=mesh['design'=8,'feat'=4] {'design'}, dimensions={0} | all-to-all | bytes 1024 | tf_op jit(solution)/shard_map/all_to_all | solution.py:59
  22.2 6.2 gather_fusion.2
  28.4 6.6 %all-to-all-start.1 = ((bf16[8,16,128,256]{3,2,1,0:T(8,128)(2,1)}), bf16[8,16,128,256]{3,2,1,0:T(8,128)(2,1)}, u32[]{:S(2)}, u32[]{:S(2)}) async-start(bf16[8,16,128,256]{3,2,1,0:T(8,128)(2,1)} %bitcast.80), calls=%async_computation.1 | async-start | bytes 16777216 | tf_op jit(solution)/shard_map/all_to_all | solution.py:67
  35.1 2.0 gather_fusion
  37.1 2.0 gather_fusion.1
  41.2 173.3 %all-to-all-done.1 = bf16[8,16,128,256]{3,2,1,0:T(8,128)(2,1)} async-done(((bf16[8,16,128,256]{3,2,1,0:T(8,128)(2,1)}), bf16[8,16,128,256]{3,2,1,0:T(8,128)(2,1)}, u32[]{:S(2)}, u32[]{:S(2)}) %all-to-all-start.1) | async-done | bytes 8388640 | tf_op jit(solution)/shard_map/all_to_all | solution.py:67
  214.5 6.2 gather_fusion.3
  220.7 7.5 %fusion.34 = f32[8192,128]{1,0:T(8,128)} fusion(bf16[8192,256]{1,0:T(8,128)(2,1)} %bitcast.72, f32[256,128]{1,0:T(8,128)S(1)} %copy-done.8), kind=kOutput, calls=%fused_computation.98 | convolution fusion | flops 3221225472 | bytes 8519680 | tf_op jit(solution)/shard_map/dot_general | solution.py:34
  228.3 95.3 %all-reduce.3.cloned.1.call-done = (f32[8192,128]{1,0:T(8,128)}, f32[512,128]{1,0:T(8,128)}, f32[512,128]{1,0:T(8,128)}) async-done(((f32[8192,128]{1,0:T(8,128)}, f32[512,128]{1,0:T(8,128)}, f32[512,128]{1,0:T(8,128)}), (f32[8192,128]{1,0:T(8,128)}, f32[512,128]{1,0:T(8,128)}, f32[512,128]{1,0:T(8,128)})) %all-reduce.3.cloned.1.call-update) | async-done | bytes 4718608 | tf_op jit(solution)/shard_map/psum | solution.py:71
  324.8 3.3 multiply_reduce_fusion.1
  328.7 7.2 %fusion = (f32[4,128]{1,0:T(4,128)S(1)}, f32[4,128,2048]{2,1,0:T(8,128)S(1)}) fusion(f32[4,2048,128]{2,1,0:T(8,128)} %bitcast.76, f32[4,2048]{1,0:T(4,128)S(1)} %sqrt.60, f32[4,128,128]{2,1,0:T(8,128)S(1)} %bitcast.81, f32[4,128]{1,0:T(4,128)S(1)} %get-tuple-element.28), kind=kOutput, calls=%fused_computation.15 | convolution fusion | flops 1613823488 | bytes 8687616 | tf_op jit(solution)/shard_map/jvp(kjc,koc->kjo)/dot_general | solution.py:21
  335.9 9.8 %multiply_reduce_fusion = (f32[4,2048]{1,0:T(4,128)S(1)}, f32[4,2048,128]{2,1,0:T(8,128)S(1)}) fusion(f32[4,2048,128]{2,1,0:T(8,128)S(1)} %bitcast.78, f32[4,2048]{1,0:T(4,128)S(1)} %multiply_divide_fusion, f32[4,128,128]{2,1,0:T(8,128)S(1)} %bitcast.82, f32[4,128]{1,0:T(4,128)S(1)} %get-tuple-element.28, f32[4,128,2048]{2,1,0:T(8,128)S(1)} %get-tuple-element.30, ...), kind=kOutput, calls=%fused_computation.11 | convolution fusion | flops 1616961536 | bytes 12914688 | tf_op jit(solution)/shard_map/transpose(jvp(kjc,koc->kjo))/dot_general | solution.py:21
  345.7 2.5 add_add_fusion
  348.3 1.9 copy-done.2
  350.2 8.9 %fusion.15 = f32[64,128,256]{2,1,0:T(8,128)} fusion(f32[64,128,128]{2,1,0:T(8,128)S(1)} %bitcast.74, f32[256,128]{1,0:T(8,128)S(1)} %copy-done.8), kind=kOutput, calls=%fused_computation.40 | convolution fusion | flops 3221225472 | bytes 12713984 | tf_op jit(solution)/shard_map/dot_general | solution.py:34
  359.1 7.8 %broadcast_in_dim.61 = f32[128,128,256]{2,1,0:T(8,128)} broadcast(f32[]{:T(128)} %constant.21.clone.1), dimensions={} | broadcast | bytes 16777220 | tf_op jit(solution)/shard_map/broadcast_in_dim | solution.py:86
  366.9 16.1 %scatter_fusion = f32[128,128,256]{2,1,0:T(8,128)} fusion(f32[128,128,256]{2,1,0:T(8,128)} %broadcast_in_dim.61, s32[64]{0:T(128)S(1)} %fusion.24, f32[64,128,256]{2,1,0:T(8,128)} %fusion.15), kind=kCustom, calls=%fused_computation.7 | custom fusion | bytes 25166080 | tf_op jit(solution)/shard_map/scatter | solution.py:86
  383.0 9.0 %convert_element_type.13 = bf16[128,128,256]{2,1,0:T(8,128)(2,1)} convert(f32[128,128,256]{2,1,0:T(8,128)} %scatter_fusion) | non-fusion elementwise | flops 4194304 | bytes 25165824 | tf_op jit(solution)/shard_map/convert_element_type | solution.py:88
  392.0 6.4 all-to-all-start.2
  399.4 7.8 %multiply_reduce_fusion.3 = (f32[4,128]{1,0:T(4,128)S(1)}, f32[4,128,128]{2,1,0:T(8,128)S(1)}) fusion(f32[4,128,128]{2,1,0:T(8,128)S(1)} %bitcast.83, f32[4,128]{1,0:T(4,128)S(1)} %multiply_divide_fusion.2, f32[4,128,128]{2,1,0:T(8,128)S(1)} %bitcast.84, f32[4,128]{1,0:T(4,128)S(1)} %get-tuple-element.24, f32[4,128]{1,0:T(4,128)S(1)} %get-tuple-element.21, ...), kind=kOutput, calls=%fused_computation.35 | convolution fusion | flops 1615199744 | bytes 9218048 | tf_op jit(solution)/shard_map/transpose(jvp(kjc,koc->kjo))/dot_general | solution.py:21
  407.5 3.6 scatter_custom_fusion.1
  411.1 6.4 scatter_custom_fusion.2
  417.6 3.5 convolution_bitcast_fusion
  421.1 5.9 convolution_add_fusion
  427.1 1.5 collective-permute-start
  428.6 39.5 %collective-permute-done = f32[256,128]{0,1:T(8,128)S(1)} collective-permute-done((f32[256,128]{0,1:T(8,128)S(1)}, f32[256,128]{0,1:T(8,128)S(1)}, u32[]{:S(2)}, u32[]{:S(2)}) %collective-permute-start) | collective-permute-done | bytes 131104 | tf_op jit(solution)/shard_map/ppermute | solution.py:108
  468.2 1.5 collective-permute-start.1
  469.6 67.6 %collective-permute-done.1 = f32[256,128]{0,1:T(8,128)S(1)} collective-permute-done((f32[256,128]{0,1:T(8,128)S(1)}, f32[256,128]{0,1:T(8,128)S(1)}, u32[]{:S(2)}, u32[]{:S(2)}) %collective-permute-start.1) | collective-permute-done | bytes 131104 | tf_op jit(solution)/shard_map/ppermute | solution.py:108
  538.1 4.9 fusion.35
  543.0 41.1 %collective-permute-done.2 = f32[256,128]{0,1:T(8,128)S(1)} collective-permute-done((f32[256,128]{0,1:T(8,128)S(1)}, f32[256,128]{0,1:T(8,128)S(1)}, u32[]{:S(2)}, u32[]{:S(2)}) %collective-permute-start.2) | collective-permute-done | bytes 131104 | tf_op jit(solution)/shard_map/ppermute | solution.py:108
  584.9 11.5 %bitcast_convert_fusion = f32[128,128,256]{2,1,0:T(8,128)} fusion(bf16[8,16,128,256]{3,2,1,0:T(8,128)(2,1)} %all-to-all-done.2), kind=kLoop, calls=%fused_computation.9 | loop fusion | flops 4194304 | bytes 25165824 | tf_op jit(solution)/shard_map/reshape | solution.py:97
  596.4 42.6 %scatter_fusion.1 = f32[32,128,256]{2,1,0:T(8,128)} fusion(f32[32,128,256]{2,1,0:T(8,128)} %bitcast.70, s32[128]{0:T(128)S(1)} %fusion.25, f32[128,128,256]{2,1,0:T(8,128)} %bitcast_convert_fusion), kind=kCustom, calls=%fused_computation.8 | custom fusion | flops 4194304 | bytes 50332160 | tf_op jit(solution)/shard_map/scatter-add | solution.py:97
  (64 shorter events, 10.8 us)
Async XLA Ops:
  7.2 15.0 %copy-start = (bf16[4096,256]{1,0:T(8,128)(2,1)S(1)}, bf16[4096,256]{1,0:T(8,128)(2,1)}, u32[]{:S(2)}) copy-start(bf16[4096,256]{1,0:T(8,128)(2,1)} %param.5) | copy-start | bytes 6291460
  28.4 6.7 %copy-start.9 = (s32[512]{0:T(512)S(1)}, s32[512]{0:T(512)}, u32[]{:S(2)}) copy-start(s32[512]{0:T(512)} %param.8) | copy-start | bytes 6148
  28.4 6.7 %copy-start.10 = (s32[512]{0:T(512)S(1)}, s32[512]{0:T(512)}, u32[]{:S(2)}) copy-start(s32[512]{0:T(512)} %param.7) | copy-start | bytes 6148
  28.4 186.1 %all-to-all-start.1 = ((bf16[8,16,128,256]{3,2,1,0:T(8,128)(2,1)}), bf16[8,16,128,256]{3,2,1,0:T(8,128)(2,1)}, u32[]{:S(2)}, u32[]{:S(2)}) async-start(bf16[8,16,128,256]{3,2,1,0:T(8,128)(2,1)} %bitcast.80), calls=%async_computation.1 | async-start | bytes 16777216 | tf_op jit(solution)/shard_map/all_to_all | solution.py:67
  35.1 4.0 copy-start.8
  35.1 288.5 %all-reduce.3.cloned.1.call-start = ((), (), s32[]{:S(2)}) async-start(), calls=%async_computation.3 | async-start | bytes 9437184 | tf_op jit(solution)/shard_map/psum | solution.py:71
  323.6 4.6 copy-start.6
  323.6 4.8 copy-start.5
  328.7 7.2 %copy-start.3 = (f32[8192,128]{1,0:T(8,128)S(1)}, f32[8192,128]{1,0:T(8,128)}, u32[]{:S(2)}) copy-start(f32[8192,128]{1,0:T(8,128)} %get-tuple-element.12) | copy-start | bytes 12582916
  335.9 9.9 %copy-start.7 = (f32[4,128,2048]{2,1,0:T(8,128)}, f32[4,128,2048]{2,1,0:T(8,128)S(1)}, u32[]{:S(2)}) copy-start(f32[4,128,2048]{2,1,0:T(8,128)S(1)} %get-tuple-element.30) | copy-start | bytes 12582916
  348.3 1.9 copy-start.2
  392.0 192.9 %all-to-all-start.2 = ((bf16[8,16,128,256]{3,2,1,0:T(8,128)(2,1)}), bf16[8,16,128,256]{3,2,1,0:T(8,128)(2,1)}, u32[]{:S(2)}, u32[]{:S(2)}) async-start(bf16[8,16,128,256]{3,2,1,0:T(8,128)(2,1)} %bitcast.79), calls=%async_computation.2 | async-start | bytes 16777216 | tf_op jit(solution)/shard_map/all_to_all | solution.py:87
  417.6 3.6 copy-start.1
  421.1 117.0 %copy-start.4 = (f32[4096,128]{1,0:T(8,128)S(1)}, f32[4096,128]{1,0:T(8,128)}, u32[]{:S(2)}) copy-start(f32[4096,128]{1,0:T(8,128)} %scatter_custom_fusion.2) | copy-start | bytes 6291460
  427.1 41.1 %collective-permute-start = (f32[256,128]{0,1:T(8,128)S(1)}, f32[256,128]{0,1:T(8,128)S(1)}, u32[]{:S(2)}, u32[]{:S(2)}) collective-permute-start(f32[256,128]{0,1:T(8,128)S(1)} %convolution_add_fusion), channel_id=1, source_target_pairs={{0,4},{4,0},{8,12},{12,8},{16,20},{20,16},{24,28},{28,24},{1,5},{5... | collective-permute-start | bytes 393224 | tf_op jit(solution)/shard_map/ppermute | solution.py:108
  468.2 69.0 %collective-permute-start.1 = (f32[256,128]{0,1:T(8,128)S(1)}, f32[256,128]{0,1:T(8,128)S(1)}, u32[]{:S(2)}, u32[]{:S(2)}) collective-permute-start(f32[256,128]{0,1:T(8,128)S(1)} %add.147), channel_id=1, source_target_pairs={{0,8},{4,12},{8,0},{12,4},{16,24},{20,28},{24,16},{28,20},{1,9},{5... | collective-permute-start | bytes 393224 | tf_op jit(solution)/shard_map/ppermute | solution.py:108
  537.2 46.9 %collective-permute-start.2 = (f32[256,128]{0,1:T(8,128)S(1)}, f32[256,128]{0,1:T(8,128)S(1)}, u32[]{:S(2)}, u32[]{:S(2)}) collective-permute-start(f32[256,128]{0,1:T(8,128)S(1)} %add.148), channel_id=1, source_target_pairs={{0,16},{4,20},{8,24},{12,28},{16,0},{20,4},{24,8},{28,12},{1,17},{... | collective-permute-start | bytes 393224 | tf_op jit(solution)/shard_map/ppermute | solution.py:108
Sparse Core Ops, SparseCore 0:
  228.4 95.0 all-reduce.2
